TPU v7x, 32 devices: a whole 2x2x4 slice. The times are simulated.
32 devices in a mesh: facet: 8 (over z, y), col: 4 (over x, core).
Axes of the slice: x: 2, y: 2, z: 4, core: 2. Of those that a mesh axis runs over, the one named last changes fastest.
Arguments:
- strip: bfloat16 [2, 64, 32768], P(None, None, 'facet'), may hold values from -6 to 6
- screen_first: bfloat16 [2, 512, 512], replicated, may hold values from -1 to 1
- screen_second: bfloat16 [2, 512, 512], replicated, may hold values from -1 to 1
- owners: int32 [4, 512, 3], P('col', 'facet'), may hold values from 0 to 15, all different within a row; in each aligned block of 64 rows (0 to 63, 64 to 127, ..., all dimensions but the last counted through in order) at most 14 rows name the same one
- live: int32 [4, 512, 3], P('col', 'facet'), may hold values 0 or 1
- place: int32 [4, 512, 3], P('col', 'facet'), may hold values from 0 to 63
Outputs:
- facet_image: float32 [2, 64, 32768], P(None, None, ('facet', 'col'))
Inputs may be any that keep to these rules, and one draw needn't show every extreme that they name: `owners`: each row names three different subgrids; among the rows of one device no subgrid is named more than 14 times, a bound that some block reaches. `place`: tile p lies at tile row p // 8 and tile column p % 8.
All inputs are finite; a program needn't handle non-finite values. No bound on the sum of `live` on one device may be relied on, other than what follows from the above.
Results may differ from a plain program's by a relative error of at most 0.013.
Values may be sent and summed in bfloat16 or wider, within the bound.
A program may use at most 64 MiB of HBM per device.

v0:
```python
import math

import functools

import jax
import jax.numpy as jnp
import numpy as np
from jax import lax
from jax.experimental import pallas as pl
from jax.experimental.pallas import tpu as pltpu
from jax.sharding import PartitionSpec as P

SUB_DEV = 2


def dft_table(length, direction):
    index = jnp.arange(length, dtype=jnp.int32)
    phase = index[:, None] * index[None, :] % length
    angle = phase.astype(jnp.float32) * (2.0 * math.pi / length)
    scale = 1.0 / math.sqrt(length)
    return (jnp.cos(angle) * scale, direction * jnp.sin(angle) * scale)


def left_apply(table, field):
    real_table, imag_table = table
    real_part, imag_part = field
    real = jnp.dot(real_table, real_part, preferred_element_type=jnp.float32) - jnp.dot(
        imag_table, imag_part, preferred_element_type=jnp.float32
    )
    imag = jnp.dot(real_table, imag_part, preferred_element_type=jnp.float32) + jnp.dot(
        imag_table, real_part, preferred_element_type=jnp.float32
    )
    return (real, imag)


def right_apply(field, table):
    real_table, imag_table = table
    real_part, imag_part = field
    real = jnp.dot(real_part, real_table, preferred_element_type=jnp.float32) - jnp.dot(
        imag_part, imag_table, preferred_element_type=jnp.float32
    )
    imag = jnp.dot(real_part, imag_table, preferred_element_type=jnp.float32) + jnp.dot(
        imag_part, real_table, preferred_element_type=jnp.float32
    )
    return (real, imag)


def screen_apply(field, screen):
    real_part, imag_part = field
    screen_real = screen[0].astype(jnp.float32)
    screen_imag = screen[1].astype(jnp.float32)
    real = real_part * screen_real - imag_part * screen_imag
    imag = real_part * screen_imag + imag_part * screen_real
    return (real.astype(jnp.bfloat16), imag.astype(jnp.bfloat16))


def process_tiles(tiles, screen_first, screen_second, forward, inverse):
    tile_count, width = tiles.shape
    side_tiles = math.isqrt(tile_count)
    win_size = math.isqrt(width // 2)
    sub_size = side_tiles * win_size
    field = (
        tiles.reshape(side_tiles, side_tiles, 2, win_size, win_size)
        .transpose(2, 0, 3, 1, 4)
        .reshape(2, sub_size, sub_size)
    )
    rows = left_apply(forward, (field[0], field[1]))
    rows = (rows[0].astype(jnp.bfloat16), rows[1].astype(jnp.bfloat16))
    spectrum = screen_apply(right_apply(rows, forward), screen_first)
    back = left_apply(inverse, spectrum)
    back = (back[0].astype(jnp.bfloat16), back[1].astype(jnp.bfloat16))
    image = screen_apply(right_apply(back, inverse), screen_second)
    stacked = jnp.stack([image[0], image[1]])
    return (
        stacked.reshape(2, side_tiles, win_size, side_tiles, win_size)
        .transpose(1, 3, 0, 2, 4)
        .reshape(tile_count, width)
    )


def exchanged(strip, screen_first, screen_second, owners, live, place):
    win_size = strip.shape[1]
    sub_size = screen_first.shape[-1]
    side_tiles = sub_size // win_size
    tile_count = side_tiles * side_tiles
    width = 2 * win_size * win_size
    peer_count = lax.axis_size("facet")
    win_local = strip.shape[2] // win_size
    sub_local = SUB_DEV
    subgrid_count = sub_local * peer_count
    capacity = max(2, (7 * win_local + 2 * subgrid_count - 1) // (2 * subgrid_count))
    total_slots = subgrid_count * capacity
    small_real, small_imag = dft_table(win_size, -1.0)
    small = (small_real.astype(jnp.bfloat16), small_imag.astype(jnp.bfloat16))
    front = left_apply(small, (strip[0], strip[1]))
    contrib = jnp.stack([front[0], front[1]]).astype(jnp.bfloat16)
    windows = (
        contrib.reshape(2, win_size, win_local, win_size)
        .transpose(2, 0, 1, 3)
        .reshape(win_local, width)
    )
    flat_owner = owners[0].reshape(-1)
    flat_live = live[0].reshape(-1)
    flat_place = place[0].reshape(-1)
    entries = flat_owner.shape[0]
    order_index = jnp.arange(entries, dtype=jnp.int32)
    earlier = (flat_owner[:, None] == flat_owner[None, :]) & (
        order_index[None, :] < order_index[:, None]
    )
    rank = jnp.sum(earlier.astype(jnp.int32), axis=1)
    slot_of = flat_owner * capacity + rank
    slot_index = jnp.arange(total_slots, dtype=jnp.int32)
    hit_rows = ((slot_of[None, :] == slot_index[:, None]) & (flat_live[None, :] == 1)).astype(
        jnp.int32
    )
    hit_cols = ((slot_of[:, None] == slot_index[None, :]) & (flat_live[:, None] == 1)).astype(
        jnp.int32
    )
    codes = jnp.sum(hit_rows * (flat_place[None, :] + 1), axis=1) - 1
    packer = jnp.sum(hit_rows.reshape(total_slots, win_local, 3), axis=2).astype(jnp.bfloat16)
    unpacker = jnp.sum(hit_cols.reshape(win_local, 3, total_slots), axis=1).astype(jnp.bfloat16)
    outgoing = jnp.dot(packer, windows, preferred_element_type=jnp.float32).astype(jnp.bfloat16)
    outgoing = outgoing.reshape(peer_count, sub_local, capacity, width)
    codes = codes.reshape(peer_count, sub_local, capacity)
    big_real, big_imag = dft_table(sub_size, -1.0)
    forward = (big_real.astype(jnp.bfloat16), big_imag.astype(jnp.bfloat16))
    inverse = (big_real.astype(jnp.bfloat16), (-big_imag).astype(jnp.bfloat16))
    tile_index = jnp.arange(tile_count, dtype=jnp.int32)
    parcels = lax.all_to_all(outgoing, "facet", split_axis=0, concat_axis=0, tiled=True)
    labels = lax.all_to_all(codes, "facet", split_axis=0, concat_axis=0, tiled=True)
    item_count = parcels.shape[1]
    sources = parcels.shape[0]
    stacked = parcels.transpose(1, 0, 2, 3).reshape(item_count, sources * capacity, width)
    marks = labels.transpose(1, 0, 2).reshape(item_count, sources * capacity)

    def one_subgrid(pair):
        slabs, tags = pair
        embed_map = (tags[None, :] == tile_index[:, None]).astype(jnp.bfloat16)
        cut_map = (tags[:, None] == tile_index[None, :]).astype(jnp.bfloat16)
        tiles = jnp.dot(embed_map, slabs, preferred_element_type=jnp.float32).astype(jnp.bfloat16)
        finished = process_tiles(tiles, screen_first, screen_second, forward, inverse)
        return jnp.dot(cut_map, finished, preferred_element_type=jnp.float32).astype(jnp.bfloat16)

    result = lax.map(one_subgrid, (stacked, marks))
    returned = lax.all_to_all(
        result.reshape(item_count, sources, capacity, width).transpose(1, 0, 2, 3),
        "facet",
        split_axis=0,
        concat_axis=0,
        tiled=True,
    )
    summed = jnp.dot(
        unpacker, returned.reshape(total_slots, width), preferred_element_type=jnp.float32
    )
    field = (
        summed.reshape(win_local, 2, win_size, win_size)
        .transpose(1, 2, 0, 3)
        .reshape(2, win_size, win_local * win_size)
    )
    column = lax.psum_scatter(
        field.astype(jnp.bfloat16), "col", scatter_dimension=2, tiled=True
    ).astype(jnp.float32)
    back_real, back_imag = dft_table(win_size, 1.0)
    highest = lax.Precision.HIGHEST
    real = jnp.dot(back_real, column[0], precision=highest) - jnp.dot(
        back_imag, column[1], precision=highest
    )
    imag = jnp.dot(back_real, column[1], precision=highest) + jnp.dot(
        back_imag, column[0], precision=highest
    )
    return jnp.stack([real, imag])


GATHER_BYTES = 16 << 20


def host_table(length):
    index = np.arange(length, dtype=np.int64)
    angle = (index[:, None] * index[None, :] % length) * (2.0 * math.pi / length)
    scale = 1.0 / math.sqrt(length)
    return np.cos(angle) * scale, -np.sin(angle) * scale


def rounded_pair(pair):
    return tuple(part.astype(jnp.bfloat16).astype(np.float64) for part in pair)


def left_block(real, imag):
    return np.concatenate(
        [np.concatenate([real, -imag], axis=1), np.concatenate([imag, real], axis=1)], axis=0
    )


def blocks_body(front_ref, big_ref, first_ref, forward_ref, inverse_ref):
    half = big_ref.shape[1]
    low, high = pl.ds(0, half), pl.ds(half, half)
    first_ref[low, low] = front_ref[0]
    first_ref[low, high] = -front_ref[1]
    first_ref[high, low] = front_ref[1]
    first_ref[high, high] = front_ref[0]
    forward_ref[low, low] = big_ref[0]
    forward_ref[low, high] = big_ref[1]
    forward_ref[high, low] = -big_ref[1]
    forward_ref[high, high] = big_ref[0]
    inverse_ref[low, low] = big_ref[0]
    inverse_ref[low, high] = -big_ref[1]
    inverse_ref[high, low] = big_ref[1]
    inverse_ref[high, high] = big_ref[0]


def table_blocks(sub_size, win_size):
    big = rounded_pair(host_table(sub_size))
    small = rounded_pair(host_table(win_size))
    eye = np.eye(sub_size // win_size)
    wide = (np.kron(eye, small[0]), np.kron(eye, small[1]))
    front = (big[0] @ wide[0] - big[1] @ wide[1], big[0] @ wide[1] + big[1] @ wide[0])
    front = np.stack(front).astype(jnp.bfloat16)
    stacked = np.stack(big).astype(jnp.bfloat16)
    full = jax.ShapeDtypeStruct((2 * sub_size, 2 * sub_size), jnp.bfloat16)
    vmem = pl.BlockSpec(memory_space=pltpu.VMEM)
    return pl.pallas_call(
        blocks_body, out_shape=[full] * 3, in_specs=[vmem] * 2, out_specs=[vmem] * 3, name="blocks"
    )(jnp.asarray(front), jnp.asarray(stacked))


def local_body(
    sub_local,
    codes_ref,
    strips_ref,
    screen_first_ref,
    screen_second_ref,
    first_ref,
    forward_ref,
    inverse_ref,
    out_ref,
    field,
    tall,
    flat,
):
    peers, _, capacity = codes_ref.shape
    win = strips_ref.shape[2]
    size = screen_first_ref.shape[1]
    tiles = size // win
    pair = 2 * win
    part_windows = out_ref.shape[3] // win
    parts = out_ref.shape[0] // peers
    base = lax.axis_index("facet") * sub_local
    lane_half = lax.broadcasted_iota(jnp.int32, (win, pair), 1) // win
    step = size // 2

    def zero_out(index, carry):
        out_ref[index] = jnp.zeros(out_ref.shape[1:], out_ref.dtype)
        return carry

    lax.fori_loop(0, out_ref.shape[0], zero_out, 0)

    def entries(subgrid, visit):
        def peer_loop(peer, carry):
            def slot_loop(slot, inner):
                code = codes_ref[peer, subgrid, slot]

                @pl.when(code >= 0)
                def _():
                    spot = code % (tiles * tiles)
                    visit(peer, code // (tiles * tiles), spot // tiles, spot % tiles)

                return inner

            return lax.fori_loop(0, capacity, slot_loop, carry)

        lax.fori_loop(0, peers, peer_loop, 0)

    def one_subgrid(number, carry):
        subgrid = base + number
        field[...] = jnp.zeros(field.shape, field.dtype)

        def embed(peer, window, row, column):
            lanes = pl.ds(pl.multiple_of(window // 2 * pair, pair), pair)
            target = pl.ds(pl.multiple_of(column // 2 * pair, pair), pair)
            shift = (window + column) % 2 * win
            for part in range(2):
                piece = strips_ref[peer, part, :, lanes].astype(jnp.float32)
                piece = pltpu.roll(piece, shift, 1)
                rows = pl.ds(pl.multiple_of(part * size + row * win, win), win)
                field[rows, target] += jnp.where(lane_half == column % 2, piece, 0.0)

        entries(subgrid, embed)
        tall[...] = field[...].astype(jnp.bfloat16)

        def left(table_ref):
            for part in range(2):
                for half in range(2):
                    rows = pl.ds(part * size + half * step, step)
                    flat[pl.ds(half * step, step), pl.ds(part * size, size)] = jnp.dot(
                        table_ref[rows, :], tall[...], preferred_element_type=jnp.float32
                    ).astype(jnp.bfloat16)

        def right(table_ref, screen_ref):
            for half in range(2):
                rows = pl.ds(half * step, step)
                product = jnp.dot(flat[rows, :], table_ref[...], preferred_element_type=jnp.float32)
                real_part, imag_part = product[:, :size], product[:, size:]
                screen_real = screen_ref[0, rows, :].astype(jnp.float32)
                screen_imag = screen_ref[1, rows, :].astype(jnp.float32)
                tall[rows, :] = (real_part * screen_real - imag_part * screen_imag).astype(
                    jnp.bfloat16
                )
                tall[pl.ds(size + half * step, step), :] = (
                    real_part * screen_imag + imag_part * screen_real
                ).astype(jnp.bfloat16)

        left(first_ref)
        right(forward_ref, screen_first_ref)
        left(forward_ref)
        right(inverse_ref, screen_second_ref)

        def cut(peer, window, row, column):
            source = pl.ds(pl.multiple_of(column // 2 * pair, pair), pair)
            spot = window % part_windows
            lanes = pl.ds(pl.multiple_of(spot // 2 * pair, pair), pair)
            slab = peer * parts + window // part_windows
            shift = (window + column) % 2 * win
            for part in range(2):
                rows = pl.ds(pl.multiple_of(part * size + row * win, win), win)
                piece = pltpu.roll(tall[rows, source].astype(jnp.float32), shift, 1)
                held = out_ref[slab, part, :, lanes].astype(jnp.float32)
                out_ref[slab, part, :, lanes] = (
                    held + jnp.where(lane_half == window % 2, piece, 0.0)
                ).astype(out_ref.dtype)

        entries(subgrid, cut)
        return carry

    lax.fori_loop(0, sub_local, one_subgrid, 0)


def entry_codes(owners, live, place, subgrid_count, tile_count):
    win_local = owners.shape[1]
    capacity = max(2, (7 * win_local + 2 * subgrid_count - 1) // (2 * subgrid_count))
    owner = owners[0].reshape(-1)
    count = owner.shape[0]
    window = jnp.arange(count, dtype=jnp.int32) // 3
    label = window * tile_count + place[0].reshape(-1) + 1
    order = jnp.arange(count, dtype=jnp.int32)
    earlier = (owner[:, None] == owner[None, :]) & (order[None, :] < order[:, None])
    rank = jnp.sum(earlier.astype(jnp.int32), axis=1)
    slot = jnp.where(live[0].reshape(-1) == 1, owner * capacity + rank, -1)
    slots = jnp.arange(subgrid_count * capacity, dtype=jnp.int32)
    hit = slot[None, :] == slots[:, None]
    codes = jnp.sum(jnp.where(hit, label[None, :], 0), axis=1) - 1
    return codes.reshape(subgrid_count, capacity)


def gathered(strip, screen_first, screen_second, owners, live, place):
    win_size = strip.shape[1]
    sub_size = screen_first.shape[-1]
    tile_count = (sub_size // win_size) ** 2
    peer_count = lax.axis_size("facet")
    parts = lax.axis_size("col")
    sub_local = SUB_DEV
    codes = entry_codes(owners, live, place, sub_local * peer_count, tile_count)
    codes = lax.all_gather(codes, "facet")
    strips = lax.all_gather(strip, "facet")
    first, forward, inverse = table_blocks(sub_size, win_size)
    piece = strip.shape[2] // parts
    vmem = pl.BlockSpec(memory_space=pltpu.VMEM)
    partial = pl.pallas_call(
        functools.partial(local_body, sub_local),
        out_shape=jax.ShapeDtypeStruct((peer_count * parts, 2, win_size, piece), jnp.bfloat16),
        in_specs=[pl.BlockSpec(memory_space=pltpu.SMEM)] + [vmem] * 6,
        out_specs=vmem,
        scratch_shapes=[
            pltpu.VMEM((2 * sub_size, sub_size), jnp.float32),
            pltpu.VMEM((2 * sub_size, sub_size), jnp.bfloat16),
            pltpu.VMEM((sub_size, 2 * sub_size), jnp.bfloat16),
        ],
        compiler_params=pltpu.CompilerParams(vmem_limit_bytes=56 << 20),
        name="local",
    )(codes, strips, screen_first, screen_second, first, forward, inverse)
    mine = lax.psum_scatter(partial, ("facet", "col"), scatter_dimension=0, tiled=True)
    return finish(mine.reshape(2 * win_size, piece), win_size)


def finish(mine, win_size):
    real, imag = host_table(win_size)
    table = jnp.asarray(left_block(real, -imag).astype(np.float32))
    image = jnp.dot(table, mine.astype(jnp.float32), precision=lax.Precision.HIGHEST)
    return image.reshape(2, win_size, mine.shape[1])


def shards(strip, screen_first, screen_second, owners, live, place):
    if strip.size * strip.dtype.itemsize * lax.axis_size("facet") <= GATHER_BYTES:
        return gathered(strip, screen_first, screen_second, owners, live, place)
    return exchanged(strip, screen_first, screen_second, owners, live, place)


def solution(mesh):
    placed = (
        P(None, None, "facet"),
        P(),
        P(),
        P("col", "facet", None),
        P("col", "facet", None),
        P("col", "facet", None),
    )
    return jax.shard_map(
        shards,
        mesh=mesh,
        in_specs=placed,
        out_specs=P(None, None, ("facet", "col")),
        check_vma=False,
    )
```

profile of v0, /device:TPU:0, one launch (start us, length us, event | category | flops | bytes accessed | tf_op | source)
XLA Modules:
  0.0 351.4 jit_solution(14555942018701495840)
XLA Ops:
  6.5 0.0 all-gather.3.cloned.1.call-start
  6.5 0.7 all-gather.3.cloned.1.call-update
  7.3 0.0 reduce-scatter.2.cloned.1.call-start
  7.3 0.7 broadcast_compare_fusion
  8.0 0.1 copy.16
  8.1 0.1 eq.37
  8.3 0.8 copy.17
  9.0 0.1 reshape_squeeze.7
  9.2 0.8 copy.18
  9.9 0.1 reshape_squeeze.8
  10.1 0.2 convert_reduce_fusion
  10.3 0.1 select_reduce_fusion
  10.4 0.1 sub.14
  10.5 4.3 %blocks.1 = (bf16[1024,1024]{1,0:T(8,128)(2,1)}, bf16[1024,1024]{1,0:T(8,128)(2,1)}, bf16[1024,1024]{1,0:T(8,128)(2,1)}) custom-call(bf16[2,512,512]{2,1,0:T(8,128)(2,1)} %constant.26.clone.front_ref, bf16[2,512,512]{2,1,0:T(8,128)(2,1)} %constant.27.clone.big_ref), custom_call_target="tpu_custom_call" | custom-call | tf_op jit(solution)/shard_map/blocks/pallas_call | solution.py:221
  14.8 35.8 %all_gather.9.codes_ref = s32[8,16,14]{2,1,0:T(8,128)} all-gather(s32[1,16,14]{2,1,0:T(8,128)S(1)} %sub.14), channel_id=1, replica_groups=mesh['facet'=8,'col'=4] {'facet'}, dimensions={0}, use_global_device_ids=true | all-gather | bytes 8064 | tf_op jit(solution)/shard_map/all_gather | solution.py:362
  50.6 86.6 %all-gather.3.cloned.1.call-done = bf16[16,64,4096]{2,1,0:T(8,128)(2,1)} async-done(((bf16[2,64,4096]{2,1,0:T(8,128)(2,1)}), bf16[16,64,4096]{2,1,0:T(8,128)(2,1)}) %all-gather.3.cloned.1.call-update) | async-done | bytes 8388624 | tf_op jit(solution)/shard_map/all_gather | solution.py:363
  137.2 46.4 %local.1 = bf16[32,2,64,1024]{3,2,1,0:T(8,128)(2,1)} custom-call(s32[8,16,14]{2,1,0:T(8,128)} %all_gather.9.codes_ref, bf16[8,2,64,4096]{3,2,1,0:T(8,128)(2,1)} %bitcast.5, bf16[2,512,512]{2,1,0:T(8,128)(2,1)} %screen_first_ref.1, bf16[2,512,512]{2,1,0:T(8,128)(2,1)} %screen_second_ref.1, bf16[1024,1024]{1,0:T(8,128)(2,1)} %get-tuple-element.8.first_ref, ...), custom_call_target="tpu_custom_call" | custom-call | tf_op jit(solution)/shard_map/local/pallas_call | solution.py:367
  183.6 0.0 copy-start
  183.6 0.0 reduce-scatter.2.cloned.1.call-update
  183.6 158.9 %reduce-scatter.2.cloned.1.call-done = bf16[1,2,64,1024]{3,2,1,0:T(8,128)(2,1)} async-done(((bf16[32,2,64,1024]{3,2,1,0:T(8,128)(2,1)}), bf16[1,2,64,1024]{3,2,1,0:T(8,128)(2,1)}) %reduce-scatter.2.cloned.1.call-update) | async-done | bytes 262160 | tf_op jit(solution)/shard_map/reduce_scatter | solution.py:380
  342.5 0.0 copy-done
  342.5 2.1 fusion.4
  (2 shorter events, 0.0 us)
Async XLA Ops:
  6.5 130.7 %all-gather.3.cloned.1.call-start = ((), (), s32[]{:S(2)}) async-start(), calls=%async_computation.2 | async-start | bytes 9437184 | tf_op jit(solution)/shard_map/all_gather | solution.py:363
  7.3 335.2 %reduce-scatter.2.cloned.1.call-start = ((), (), s32[]{:S(2)}) async-start(), calls=%async_computation.1 | async-start | bytes 8650752 | tf_op jit(solution)/shard_map/reduce_scatter | solution.py:380
  183.6 158.9 %copy-start = (f32[128,128]{1,0:T(8,128)S(1)}, f32[128,128]{1,0:T(8,128)}, u32[]{:S(2)}) copy-start(f32[128,128]{1,0:T(8,128)} %constant.28.clone) | copy-start | bytes 196612
Sparse Core Ops, SparseCore 0:
  9.5 127.7 all-gather.2
  183.7 158.7 reduce-scatter.1
where the time goes:
time: 352 us; the launch traced here: 351 us
  waiting for transfers between devices  246 us (70%)
  Pallas kernels  50.7 us (14%)
  blocking collectives  35.8 us (10%)
  between operations  13.4 us (4%)
    reduce_scatter x1, waiting for transfers between devices, gathered(): lax.psum_scatter(partial, ('facet', 'col'), scatter_dimension=0, tiled=True)  159 us
    all_gather x1, waiting for transfers between devices, gathered(): strips = lax.all_gather(strip, 'facet')  86.6 us
    pallas_call x1, Pallas kernels, gathered(): pl.pallas_call(functools.partial(local_body, sub_local), out_shape=jax.Sh...  46.4 us
    all_gather x1, blocking collectives, gathered(): codes = lax.all_gather(codes, 'facet')  35.8 us
  transfers between devices with their start and end apart: 2, of which 2 were waited for; matrix products, arithmetic and copies ran while one was open for 1% of the time, Pallas kernels for 1%

commit v1 on v0

--- a/solution.py
+++ b/solution.py
@@ -191,7 +191,7 @@
     )
 
 
-def blocks_body(front_ref, big_ref, first_ref, forward_ref, inverse_ref):
+def fill_blocks(front_ref, big_ref, first_ref, forward_ref, inverse_ref):
     half = big_ref.shape[1]
     low, high = pl.ds(0, half), pl.ds(half, half)
     first_ref[low, low] = front_ref[0]
@@ -208,23 +208,356 @@
     inverse_ref[high, high] = big_ref[0]
 
 
-def table_blocks(sub_size, win_size):
+def table_pairs(sub_size, win_size):
     big = rounded_pair(host_table(sub_size))
     small = rounded_pair(host_table(win_size))
     eye = np.eye(sub_size // win_size)
     wide = (np.kron(eye, small[0]), np.kron(eye, small[1]))
     front = (big[0] @ wide[0] - big[1] @ wide[1], big[0] @ wide[1] + big[1] @ wide[0])
-    front = np.stack(front).astype(jnp.bfloat16)
-    stacked = np.stack(big).astype(jnp.bfloat16)
-    full = jax.ShapeDtypeStruct((2 * sub_size, 2 * sub_size), jnp.bfloat16)
+    return np.stack(front).astype(jnp.bfloat16), np.stack(big).astype(jnp.bfloat16)
+
+
+def meet(partners):
+    barrier = pltpu.get_barrier_semaphore()
+    for partner in partners:
+        pl.semaphore_signal(
+            barrier, inc=1, device_id=partner, device_id_type=pl.DeviceIdType.MESH
+        )
+    pl.semaphore_wait(barrier, len(partners))
+
+
+def gather_body(
+    peers,
+    strip_ref,
+    codes_ref,
+    front_ref,
+    big_ref,
+    out_ref,
+    all_codes_ref,
+    first_out,
+    forward_out,
+    inverse_out,
+    first_ref,
+    forward_ref,
+    inverse_ref,
+    send_sem,
+    recv_sem,
+    code_send,
+    code_recv,
+    local_sem,
+):
+    levels = peers // 2
+    facet, col = lax.axis_index("facet"), lax.axis_index("col")
+    z, y = facet // 2, facet % 2
+    x, core = col // 2, col % 2
+    half = strip_ref.shape[1] // 2
+    higher = [lax.rem(z + d, levels) for d in range(1, levels)]
+    z_peers = [(level * 2 + y, col) for level in higher]
+    y_peer = (z * 2 + 1 - y, col)
+    x_peer = (facet, (1 - x) * 2 + core)
+    core_peer = (facet, x * 2 + 1 - core)
+    corners = [(level * 2 + 1 - y, col) for level in higher]
+    meet(z_peers + [y_peer, x_peer, core_peer] + corners)
+    started = []
+
+    def piece(ref, x_at, core_at):
+        return ref.at[x_at, pl.ds(pl.multiple_of(core_at * half, half), half)]
+
+    def send(source, item, x_at, core_at, kind, target):
+        copy = pltpu.make_async_remote_copy(
+            src_ref=piece(source, x_at, core_at),
+            dst_ref=piece(out_ref.at[item], x_at, core_at),
+            send_sem=send_sem.at[len(started)],
+            recv_sem=recv_sem.at[kind, item],
+            device_id=target,
+            device_id_type=pl.DeviceIdType.MESH,
+        )
+        copy.start()
+        started.append(copy)
+
+    def arrived(item, x_at, core_at, kind):
+        pltpu.make_async_copy(
+            piece(out_ref.at[item], x_at, core_at),
+            piece(out_ref.at[item], x_at, core_at),
+            recv_sem.at[kind, item],
+        ).wait()
+
+    send(strip_ref, facet, x, core, 0, y_peer)
+    for target in z_peers:
+        send(strip_ref, facet, x, core, 0, target)
+    codes_sent = []
+    for number, target in enumerate([y_peer] + z_peers + corners):
+        copy = pltpu.make_async_remote_copy(
+            src_ref=codes_ref,
+            dst_ref=all_codes_ref.at[facet],
+            send_sem=code_send.at[number],
+            recv_sem=code_recv.at[facet],
+            device_id=target,
+            device_id_type=pl.DeviceIdType.MESH,
+        )
+        copy.start()
+        codes_sent.append(copy)
+    kept = [
+        pltpu.make_async_copy(strip_ref, out_ref.at[facet], local_sem.at[0]),
+        pltpu.make_async_copy(codes_ref, all_codes_ref.at[facet], local_sem.at[1]),
+    ]
+    for copy in kept:
+        copy.start()
+    fill_blocks(front_ref, big_ref, first_ref, forward_ref, inverse_ref)
+    for number, (source, target) in enumerate(
+        [(first_ref, first_out), (forward_ref, forward_out), (inverse_ref, inverse_out)]
+    ):
+        copy = pltpu.make_async_copy(source, target, local_sem.at[2 + number])
+        copy.start()
+        kept.append(copy)
+
+    def pass_on(item, kind, x_at):
+        arrived(item, x_at, core, kind)
+        send(out_ref.at[item], item, x_at, core, kind + 2, core_peer)
+
+    order = [z] + higher
+    for number, level in enumerate(order):
+        same, other = level * 2 + y, level * 2 + 1 - y
+        if number > 0:
+            arrived(same, x, core, 0)
+            send(out_ref.at[same], same, x, core, 0, y_peer)
+            send(out_ref.at[same], same, x, core, 1, x_peer)
+            send(out_ref.at[same], same, x, core, 2, core_peer)
+        arrived(other, x, core, 0)
+        send(out_ref.at[other], other, x, core, 1, x_peer)
+        send(out_ref.at[other], other, x, core, 2, core_peer)
+    for number, level in enumerate(order):
+        if number > 0:
+            pass_on(level * 2 + y, 1, 1 - x)
+        pass_on(level * 2 + 1 - y, 1, 1 - x)
+    for number, level in enumerate(order):
+        for item in [level * 2 + y, level * 2 + 1 - y][number == 0 :]:
+            arrived(item, x, 1 - core, 2)
+            arrived(item, 1 - x, 1 - core, 3)
+            pltpu.make_async_copy(
+                all_codes_ref.at[item], all_codes_ref.at[item], code_recv.at[item]
+            ).wait()
+    for copy in started + codes_sent:
+        copy.wait_send()
+    for copy in kept:
+        copy.wait()
+
+
+def gather_strips(strip, codes, peers, sub_size, win_size):
+    front, big = table_pairs(sub_size, win_size)
+    full = (2 * sub_size, 2 * sub_size)
+    lanes = 128
+    padded = jnp.pad(codes, ((0, 0), (0, lanes - codes.shape[1])), constant_values=-1)
     vmem = pl.BlockSpec(memory_space=pltpu.VMEM)
+    anywhere = pl.BlockSpec(memory_space=pl.ANY)
+    levels = peers // 2
+    copies = levels + 3 * (levels - 1) + 2 * levels + 2 * levels - 1
     return pl.pallas_call(
-        blocks_body, out_shape=[full] * 3, in_specs=[vmem] * 2, out_specs=[vmem] * 3, name="blocks"
-    )(jnp.asarray(front), jnp.asarray(stacked))
+        functools.partial(gather_body, peers),
+        out_shape=[
+            jax.ShapeDtypeStruct((peers,) + strip.shape, strip.dtype),
+            jax.ShapeDtypeStruct((peers,) + padded.shape, padded.dtype),
+        ]
+        + [jax.ShapeDtypeStruct(full, jnp.bfloat16)] * 3,
+        in_specs=[vmem] * 4,
+        out_specs=[anywhere] * 5,
+        scratch_shapes=[pltpu.VMEM(full, jnp.bfloat16)] * 3
+        + [
+            pltpu.SemaphoreType.DMA((copies,)),
+            pltpu.SemaphoreType.DMA((4, peers)),
+            pltpu.SemaphoreType.DMA((peers,)),
+            pltpu.SemaphoreType.DMA((peers,)),
+            pltpu.SemaphoreType.DMA((5,)),
+        ],
+        compiler_params=pltpu.CompilerParams(collective_id=0, has_side_effects=True),
+        name="gather",
+    )(strip, padded, jnp.asarray(front), jnp.asarray(big))
+
+
+def reduce_body(
+    levels,
+    partial_ref,
+    out_ref,
+    held,
+    from_core,
+    from_x_wide,
+    from_y_wide,
+    from_y,
+    from_x,
+    done,
+    from_z,
+    send_sem,
+    recv_sem,
+    z_send,
+    z_recv,
+    local_sem,
+):
+    facet, col = lax.axis_index("facet"), lax.axis_index("col")
+    z, y = facet // 2, facet % 2
+    x, core = col // 2, col % 2
+    half = out_ref.shape[1] // 2
+    top, bottom = pl.ds(0, half), pl.ds(half, half)
+    order = [lax.rem(z + d, levels) for d in range(1, levels)] + [z]
+    z_peers = [(level * 2 + y, col) for level in order[:-1]]
+    y_peer = (z * 2 + 1 - y, col)
+    x_peer = (facet, (1 - x) * 2 + core)
+    core_peer = (facet, x * 2 + 1 - core)
+    meet(z_peers + [y_peer, x_peer, core_peer])
+    sent = []
+
+    def send(source, target, kind, number, peer):
+        copy = pltpu.make_async_remote_copy(
+            src_ref=source,
+            dst_ref=target,
+            send_sem=send_sem.at[kind, number],
+            recv_sem=recv_sem.at[kind, number],
+            device_id=peer,
+            device_id_type=pl.DeviceIdType.MESH,
+        )
+        copy.start()
+        sent.append(copy)
+        return copy
+
+    def add(target, left, right):
+        target[...] = (left[...].astype(jnp.float32) + right[...].astype(jnp.float32)).astype(
+            target.dtype
+        )
+
+    first, kept = [], []
+    for number, level in enumerate(order):
+        first.append(
+            send(partial_ref.at[1 - core, level], from_core.at[number], 0, number, core_peer)
+        )
+        copy = pltpu.make_async_copy(
+            partial_ref.at[core, level], held.at[number], local_sem.at[number]
+        )
+        copy.start()
+        kept.append(copy)
+    wide_x, wide_y, narrow_x, narrow_y, across = [], [], [], [], []
+
+    def join_cores(number):
+        kept[number].wait()
+        first[number].wait_recv()
+
+        def body(index, carry):
+            y_at, x_at, part = index // 4, index // 2 % 2, index % 2
+            add(
+                held.at[number, y_at, x_at, part],
+                held.at[number, y_at, x_at, part],
+                from_core.at[number, y_at, x_at, part],
+            )
+            return carry
+
+        lax.fori_loop(0, 8, body, 0)
+        wide_x.append(
+            send(held.at[number, :, 1 - x, :, top], from_x_wide.at[number], 1, number, x_peer)
+        )
+        wide_y.append(
+            send(held.at[number, 1 - y, :, :, bottom], from_y_wide.at[number], 2, number, y_peer)
+        )
+
+    def join_wide(number):
+        wide_x[number].wait_recv()
+
+        def body_x(index, carry):
+            place = held.at[number, index // 2, x, index % 2, top]
+            add(place, place, from_x_wide.at[number, index // 2, index % 2])
+            return carry
+
+        lax.fori_loop(0, 4, body_x, 0)
+        narrow_y.append(
+            send(held.at[number, 1 - y, x, :, top], from_y.at[number], 3, number, y_peer)
+        )
+        wide_y[number].wait_recv()
+
+        def body_y(index, carry):
+            place = held.at[number, y, index // 2, index % 2, bottom]
+            add(place, place, from_y_wide.at[number, index // 2, index % 2])
+            return carry
+
+        lax.fori_loop(0, 4, body_y, 0)
+        narrow_x.append(
+            send(held.at[number, y, 1 - x, :, bottom], from_x.at[number], 4, number, x_peer)
+        )
+
+    def join_narrow(number):
+        narrow_y[number].wait_recv()
+        for part in range(2):
+            add(
+                done.at[number, part, top],
+                held.at[number, y, x, part, top],
+                from_y.at[number, part],
+            )
+        narrow_x[number].wait_recv()
+        for part in range(2):
+            add(
+                done.at[number, part, bottom],
+                held.at[number, y, x, part, bottom],
+                from_x.at[number, part],
+            )
+        if number < levels - 1:
+            copy = pltpu.make_async_remote_copy(
+                src_ref=done.at[number],
+                dst_ref=from_z.at[number],
+                send_sem=z_send.at[number],
+                recv_sem=z_recv.at[number],
+                device_id=z_peers[number],
+                device_id_type=pl.DeviceIdType.MESH,
+            )
+            copy.start()
+            across.append(copy)
+
+    for step in range(levels + 2):
+        if step < levels:
+            join_cores(step)
+        if 0 <= step - 1 < levels:
+            join_wide(step - 1)
+        if 0 <= step - 2 < levels:
+            join_narrow(step - 2)
+    for copy in across:
+        copy.wait_recv()
+    for part in range(2):
+        total = done[levels - 1, part].astype(jnp.float32)
+        for number in range(levels - 1):
+            total += from_z[number, part].astype(jnp.float32)
+        out_ref[part] = total
+    for copy in sent + across:
+        copy.wait_send()
+
+
+def reduce_partials(partial, levels, win_size, width):
+    kind = partial.dtype
+    half = win_size // 2
+    return pl.pallas_call(
+        functools.partial(reduce_body, levels),
+        out_shape=jax.ShapeDtypeStruct((2, win_size, width), jnp.float32),
+        in_specs=[pl.BlockSpec(memory_space=pl.ANY)],
+        out_specs=pl.BlockSpec(memory_space=pltpu.VMEM),
+        scratch_shapes=[
+            pltpu.VMEM((levels, 2, 2, 2, win_size, width), kind),
+            pltpu.VMEM((levels, 2, 2, 2, win_size, width), kind),
+            pltpu.VMEM((levels, 2, 2, half, width), kind),
+            pltpu.VMEM((levels, 2, 2, half, width), kind),
+            pltpu.VMEM((levels, 2, half, width), kind),
+            pltpu.VMEM((levels, 2, half, width), kind),
+            pltpu.VMEM((levels, 2, win_size, width), kind),
+            pltpu.VMEM((levels - 1, 2, win_size, width), kind),
+            pltpu.SemaphoreType.DMA((5, levels)),
+            pltpu.SemaphoreType.DMA((5, levels)),
+            pltpu.SemaphoreType.DMA((levels - 1,)),
+            pltpu.SemaphoreType.DMA((levels - 1,)),
+            pltpu.SemaphoreType.DMA((levels,)),
+        ],
+        compiler_params=pltpu.CompilerParams(
+            collective_id=1, has_side_effects=True, vmem_limit_bytes=40 << 20
+        ),
+        name="reduce",
+    )(partial.reshape(2, levels, 2, 2, 2, win_size, width))
 
 
 def local_body(
     sub_local,
+    capacity,
     codes_ref,
     strips_ref,
     screen_first_ref,
@@ -237,7 +570,7 @@
     tall,
     flat,
 ):
-    peers, _, capacity = codes_ref.shape
+    peers = codes_ref.shape[0]
     win = strips_ref.shape[2]
     size = screen_first_ref.shape[1]
     tiles = size // win
@@ -318,7 +651,8 @@
             source = pl.ds(pl.multiple_of(column // 2 * pair, pair), pair)
             spot = window % part_windows
             lanes = pl.ds(pl.multiple_of(spot // 2 * pair, pair), pair)
-            slab = peer * parts + window // part_windows
+            part_index = window // part_windows
+            slab = (part_index % 2 * peers + peer) * (parts // 2) + part_index // 2
             shift = (window + column) % 2 * win
             for part in range(2):
                 rows = pl.ds(pl.multiple_of(part * size + row * win, win), win)
@@ -359,13 +693,14 @@
     parts = lax.axis_size("col")
     sub_local = SUB_DEV
     codes = entry_codes(owners, live, place, sub_local * peer_count, tile_count)
-    codes = lax.all_gather(codes, "facet")
-    strips = lax.all_gather(strip, "facet")
-    first, forward, inverse = table_blocks(sub_size, win_size)
+    capacity = codes.shape[1]
+    strips, codes, first, forward, inverse = gather_strips(
+        strip, codes, peer_count, sub_size, win_size
+    )
     piece = strip.shape[2] // parts
     vmem = pl.BlockSpec(memory_space=pltpu.VMEM)
     partial = pl.pallas_call(
-        functools.partial(local_body, sub_local),
+        functools.partial(local_body, sub_local, capacity),
         out_shape=jax.ShapeDtypeStruct((peer_count * parts, 2, win_size, piece), jnp.bfloat16),
         in_specs=[pl.BlockSpec(memory_space=pltpu.SMEM)] + [vmem] * 6,
         out_specs=vmem,
@@ -377,19 +712,20 @@
         compiler_params=pltpu.CompilerParams(vmem_limit_bytes=56 << 20),
         name="local",
     )(codes, strips, screen_first, screen_second, first, forward, inverse)
-    mine = lax.psum_scatter(partial, ("facet", "col"), scatter_dimension=0, tiled=True)
+    mine = reduce_partials(partial, peer_count // 2, win_size, piece)
     return finish(mine.reshape(2 * win_size, piece), win_size)
 
 
 def finish(mine, win_size):
     real, imag = host_table(win_size)
     table = jnp.asarray(left_block(real, -imag).astype(np.float32))
-    image = jnp.dot(table, mine.astype(jnp.float32), precision=lax.Precision.HIGHEST)
+    image = jnp.dot(table, mine, precision=lax.Precision.HIGHEST)
     return image.reshape(2, win_size, mine.shape[1])
 
 
 def shards(strip, screen_first, screen_second, owners, live, place):
-    if strip.size * strip.dtype.itemsize * lax.axis_size("facet") <= GATHER_BYTES:
+    paired = lax.axis_size("facet") % 2 == 0 and lax.axis_size("col") == 4
+    if paired and strip.size * strip.dtype.itemsize * lax.axis_size("facet") <= GATHER_BYTES:
         return gathered(strip, screen_first, screen_second, owners, live, place)
     return exchanged(strip, screen_first, screen_second, owners, live, place)
 

time: 352 us -> 181 us (0.51)
  waiting for transfers between devices: 246 us -> 0 us
  Pallas kernels: 50.7 us -> 172 us
  blocking collectives: 35.8 us -> 0 us
  between operations: 13.4 us -> 0.05 us
  local copies, waits for them, and re-layouts: 2.16 us -> 6.16 us
    reduce_scatter x1 -> x0, waiting for transfers between devices: 159 us -> none  [gathered(): lax.psum_scatter(partial, ('facet', 'col'), scatter_dimension=0, tiled=True)]
    pallas_call x2 -> x3, Pallas kernels: 50.7 us -> 172 us  [the longest x1 61.1 us: gather_strips(): pl.pallas_call(functools.partial(gather_body, peers), out_shape=[jax.Shap...]
    all_gather x1 -> x0, waiting for transfers between devices: 86.6 us -> none  [gathered(): strips = lax.all_gather(strip, 'facet')]
    all_gather x1 -> x0, blocking collectives: 35.8 us -> none  [gathered(): codes = lax.all_gather(codes, 'facet')]
  transfers between devices with their start and end apart: 2 -> 0, of which waited for: 2 -> 0; matrix products, arithmetic and copies ran while one was open for 1% -> 0% of each run, Pallas kernels for 1% -> 0%
where the time goes in v1:
time: 181 us; the launch traced here: 180 us
  Pallas kernels  172 us (95%)
  local copies, waits for them, and re-layouts  6.16 us (3%)
    pallas_call x1, Pallas kernels, gather_strips(): pl.pallas_call(functools.partial(gather_body, peers), out_shape=[jax.Shap...  61.1 us
    pallas_call x1, Pallas kernels, gathered(): pl.pallas_call(functools.partial(local_body, sub_local, capacity), out_sh...  57.3 us
    pallas_call x1, Pallas kernels, reduce_partials(): pl.pallas_call(functools.partial(reduce_body, levels), out_shape=jax.Shap...  53.3 us
    unnamed x6, local copies, waits for them, and re-layouts  4.93 us

profile of v1, /device:TPU:0, one launch (start us, length us, event | category | flops | bytes accessed | tf_op | source)
XLA Modules:
  0.0 180.4 jit_solution(4629200600518146478)
XLA Ops:
  0.0 0.7 broadcast_compare_fusion
  0.7 0.1 copy.13
  0.8 0.1 eq.37
  1.0 0.8 copy.14
  1.7 0.1 reshape_squeeze.7
  1.9 0.2 convert_reduce_fusion
  2.1 0.8 copy.15
  2.8 0.1 reshape_squeeze.8
  3.0 0.1 select_reduce_fusion
  3.1 0.1 sub.14
  3.2 0.6 pad.4.codes_ref
  3.8 61.1 %gather.1 = (bf16[8,2,64,4096]{3,2,1,0:T(8,128)(2,1)}, s32[8,16,128]{2,1,0:T(8,128)}, bf16[1024,1024]{1,0:T(8,128)(2,1)}, bf16[1024,1024]{1,0:T(8,128)(2,1)}, bf16[1024,1024]{1,0:T(8,128)(2,1)}) custom-call(bf16[2,64,4096]{2,1,0:T(8,128)(2,1)} %strip_ref.1, s32[16,128]{1,0:T(8,128)} %pad.4.codes_ref, bf16[2,512,512]{2,1,0:T(8,128)(2,1)} %constant.26.clone.front_ref, ...), custom_call_target="tpu_custom_call" | custom-call | tf_op jit(solution)/shard_map/gather/pallas_call | solution.py:355
  64.9 57.3 %local.1 = bf16[32,2,64,1024]{3,2,1,0:T(8,128)(2,1)} custom-call(s32[8,16,128]{2,1,0:T(8,128)} %get-tuple-element.10.codes_ref, bf16[8,2,64,4096]{3,2,1,0:T(8,128)(2,1)} %get-tuple-element.11.strips_ref, bf16[2,512,512]{2,1,0:T(8,128)(2,1)} %screen_first_ref.1, bf16[2,512,512]{2,1,0:T(8,128)(2,1)} %screen_second_ref.1, ...), custom_call_target="tpu_custom_call" | custom-call | tf_op jit(solution)/shard_map/local/pallas_call | solution.py:702
  122.3 0.0 copy-start
  122.3 3.4 %copy-done = bf16[32,2,64,1024]{3,2,1,0:T(8,128)(2,1)S(1)} copy-done((bf16[32,2,64,1024]{3,2,1,0:T(8,128)(2,1)S(1)}, bf16[32,2,64,1024]{3,2,1,0:T(8,128)(2,1)}, u32[]{:S(2)}) %copy-start) | copy-done | bytes 8388632
  125.7 0.0 copy-start.1
  125.7 53.3 %reduce.1 = f32[2,64,1024]{2,1,0:T(8,128)S(1)} custom-call(bf16[2,4,2,2,2,64,1024]{6,5,4,3,2,1,0:T(8,128)(2,1)S(1)} %bitcast.5), custom_call_target="tpu_custom_call" | custom-call | tf_op jit(solution)/shard_map/reduce/pallas_call | solution.py:531
  179.0 0.0 copy-done.1
  179.0 1.4 fusion.4
  (2 shorter events, 0.0 us)
Async XLA Ops:
  122.3 3.4 %copy-start = (bf16[32,2,64,1024]{3,2,1,0:T(8,128)(2,1)S(1)}, bf16[32,2,64,1024]{3,2,1,0:T(8,128)(2,1)}, u32[]{:S(2)}) copy-start(bf16[32,2,64,1024]{3,2,1,0:T(8,128)(2,1)} %local.1) | copy-start | bytes 25165828
  125.7 53.3 %copy-start.1 = (f32[128,128]{1,0:T(8,128)S(1)}, f32[128,128]{1,0:T(8,128)}, u32[]{:S(2)}) copy-start(f32[128,128]{1,0:T(8,128)} %constant.28.clone) | copy-start | bytes 196612

commit v2 on v1

--- a/solution.py
+++ b/solution.py
@@ -172,6 +172,7 @@
 
 
 GATHER_BYTES = 16 << 20
+UNROLL = 4
 
 
 def host_table(length):
@@ -549,16 +550,29 @@
             pltpu.SemaphoreType.DMA((levels,)),
         ],
         compiler_params=pltpu.CompilerParams(
-            collective_id=1, has_side_effects=True, vmem_limit_bytes=40 << 20
+            collective_id=1, has_side_effects=True, vmem_limit_bytes=60 << 20
         ),
         name="reduce",
     )(partial.reshape(2, levels, 2, 2, 2, win_size, width))
+
+
+def parted(value, count):
+    if count & (count - 1) == 0:
+        return lax.shift_right_logical(value, count.bit_length() - 1), value & (count - 1)
+    return lax.div(value, count), lax.rem(value, count)
 
 
 def local_body(
     sub_local,
     capacity,
     codes_ref,
+    strips_hbm,
+    screen_first_hbm,
+    screen_second_hbm,
+    first_hbm,
+    forward_hbm,
+    inverse_hbm,
+    out_hbm,
     strips_ref,
     screen_first_ref,
     screen_second_ref,
@@ -567,11 +581,16 @@
     inverse_ref,
     out_ref,
     field,
-    tall,
+    tall_all,
     flat,
+    listed,
+    strip_sem,
+    table_sem,
+    out_sem,
 ):
     peers = codes_ref.shape[0]
     win = strips_ref.shape[2]
+    win_local = strips_ref.shape[3] // win
     size = screen_first_ref.shape[1]
     tiles = size // win
     pair = 2 * win
@@ -580,6 +599,24 @@
     base = lax.axis_index("facet") * sub_local
     lane_half = lax.broadcasted_iota(jnp.int32, (win, pair), 1) // win
     step = size // 2
+    loads = [
+        pltpu.make_async_copy(strips_hbm.at[peer], strips_ref.at[peer], strip_sem.at[peer])
+        for peer in range(peers)
+    ]
+    tables = [
+        pltpu.make_async_copy(source, target, table_sem.at[number])
+        for number, (source, target) in enumerate(
+            [
+                (first_hbm, first_ref),
+                (forward_hbm, forward_ref),
+                (screen_first_hbm, screen_first_ref),
+                (inverse_hbm, inverse_ref),
+                (screen_second_hbm, screen_second_ref),
+            ]
+        )
+    ]
+    for copy in loads + tables:
+        copy.start()
 
     def zero_out(index, carry):
         out_ref[index] = jnp.zeros(out_ref.shape[1:], out_ref.dtype)
@@ -587,38 +624,63 @@
 
     lax.fori_loop(0, out_ref.shape[0], zero_out, 0)
 
-    def entries(subgrid, visit):
-        def peer_loop(peer, carry):
-            def slot_loop(slot, inner):
-                code = codes_ref[peer, subgrid, slot]
-
-                @pl.when(code >= 0)
-                def _():
-                    spot = code % (tiles * tiles)
-                    visit(peer, code // (tiles * tiles), spot // tiles, spot % tiles)
-
-                return inner
-
-            return lax.fori_loop(0, capacity, slot_loop, carry)
-
-        lax.fori_loop(0, peers, peer_loop, 0)
-
-    def one_subgrid(number, carry):
-        subgrid = base + number
+    def list_up(number):
+        def peer_loop(peer, count):
+            for slot in range(capacity):
+                code = codes_ref[peer, base + number, slot]
+                listed[number, count] = peer * (win_local * tiles * tiles) + code
+                count += (code >= 0).astype(jnp.int32)
+            return count
+
+        count = lax.fori_loop(0, peers, peer_loop, 0)
+        for extra in range(UNROLL):
+            listed[number, count + extra] = -1
+        return lax.div(count + UNROLL - 1, UNROLL)
+
+    rounds = [list_up(number) for number in range(sub_local)]
+
+    def entry(number, index):
+        value = listed[number, index]
+        code = jnp.maximum(value, 0)
+        peer, rest = parted(code, win_local * tiles * tiles)
+        window, spot = parted(rest, tiles * tiles)
+        row, column = parted(spot, tiles)
+        return value >= 0, peer, window, row, column
+
+    def embed_all(number):
         field[...] = jnp.zeros(field.shape, field.dtype)
 
-        def embed(peer, window, row, column):
-            lanes = pl.ds(pl.multiple_of(window // 2 * pair, pair), pair)
-            target = pl.ds(pl.multiple_of(column // 2 * pair, pair), pair)
-            shift = (window + column) % 2 * win
-            for part in range(2):
-                piece = strips_ref[peer, part, :, lanes].astype(jnp.float32)
-                piece = pltpu.roll(piece, shift, 1)
-                rows = pl.ds(pl.multiple_of(part * size + row * win, win), win)
-                field[rows, target] += jnp.where(lane_half == column % 2, piece, 0.0)
-
-        entries(subgrid, embed)
-        tall[...] = field[...].astype(jnp.bfloat16)
+        def body(turn, carry):
+            todo = []
+            for extra in range(UNROLL):
+                valid, peer, window, row, column = entry(number, turn * UNROLL + extra)
+                at, odd = parted(window, 2)
+                lanes = pl.ds(pl.multiple_of(at * pair, pair), pair)
+                at, column_odd = parted(column, 2)
+                target = pl.ds(pl.multiple_of(at * pair, pair), pair)
+                chosen = lane_half == jnp.where(valid, column_odd, 2)
+                shift = (odd ^ column_odd) * win
+                for part in range(2):
+                    piece = strips_ref[peer, part, :, lanes].astype(jnp.float32)
+                    piece = jnp.where(chosen, pltpu.roll(piece, shift, 1), 0.0)
+                    rows = pl.ds(pl.multiple_of(part * size + row * win, win), win)
+                    todo.append((rows, target, piece))
+            for rows, target, piece in todo:
+                field[rows, target] += piece
+            return carry
+
+        lax.fori_loop(0, rounds[number], body, 0)
+        tall_all[number] = field[...].astype(jnp.bfloat16)
+
+    for copy in loads:
+        copy.wait()
+    for number in range(sub_local):
+        embed_all(number)
+    for copy in tables:
+        copy.wait()
+
+    def transform(number, carry):
+        tall = tall_all.at[number]
 
         def left(table_ref):
             for part in range(2):
@@ -646,26 +708,41 @@
         right(forward_ref, screen_first_ref)
         left(forward_ref)
         right(inverse_ref, screen_second_ref)
-
-        def cut(peer, window, row, column):
-            source = pl.ds(pl.multiple_of(column // 2 * pair, pair), pair)
-            spot = window % part_windows
-            lanes = pl.ds(pl.multiple_of(spot // 2 * pair, pair), pair)
-            part_index = window // part_windows
-            slab = (part_index % 2 * peers + peer) * (parts // 2) + part_index // 2
-            shift = (window + column) % 2 * win
-            for part in range(2):
-                rows = pl.ds(pl.multiple_of(part * size + row * win, win), win)
-                piece = pltpu.roll(tall[rows, source].astype(jnp.float32), shift, 1)
+        return carry
+
+    lax.fori_loop(0, sub_local, transform, 0)
+
+    def cut_all(number):
+        def body(turn, carry):
+            todo = []
+            for extra in range(UNROLL):
+                valid, peer, window, row, column = entry(number, turn * UNROLL + extra)
+                at, column_odd = parted(column, 2)
+                source = pl.ds(pl.multiple_of(at * pair, pair), pair)
+                part_index, spot = parted(window, part_windows)
+                at, odd = parted(spot, 2)
+                lanes = pl.ds(pl.multiple_of(at * pair, pair), pair)
+                outer, inner = parted(part_index, 2)
+                slab = (inner * peers + peer) * (parts // 2) + outer
+                chosen = lane_half == jnp.where(valid, odd, 2)
+                shift = (odd ^ column_odd) * win
+                for part in range(2):
+                    rows = pl.ds(pl.multiple_of(part * size + row * win, win), win)
+                    piece = tall_all[number, rows, source].astype(jnp.float32)
+                    piece = jnp.where(chosen, pltpu.roll(piece, shift, 1), 0.0)
+                    todo.append((slab, part, lanes, piece))
+            for slab, part, lanes, piece in todo:
                 held = out_ref[slab, part, :, lanes].astype(jnp.float32)
-                out_ref[slab, part, :, lanes] = (
-                    held + jnp.where(lane_half == window % 2, piece, 0.0)
-                ).astype(out_ref.dtype)
-
-        entries(subgrid, cut)
-        return carry
-
-    lax.fori_loop(0, sub_local, one_subgrid, 0)
+                out_ref[slab, part, :, lanes] = (held + piece).astype(out_ref.dtype)
+            return carry
+
+        lax.fori_loop(0, rounds[number], body, 0)
+
+    for number in range(sub_local):
+        cut_all(number)
+    copy = pltpu.make_async_copy(out_ref, out_hbm, out_sem)
+    copy.start()
+    copy.wait()
 
 
 def entry_codes(owners, live, place, subgrid_count, tile_count):
@@ -698,18 +775,29 @@
         strip, codes, peer_count, sub_size, win_size
     )
     piece = strip.shape[2] // parts
-    vmem = pl.BlockSpec(memory_space=pltpu.VMEM)
+    anywhere = pl.BlockSpec(memory_space=pl.ANY)
+    slabs = (peer_count * parts, 2, win_size, piece)
+    listing = -(-(peer_count * capacity + UNROLL) // 128) * 128
     partial = pl.pallas_call(
         functools.partial(local_body, sub_local, capacity),
-        out_shape=jax.ShapeDtypeStruct((peer_count * parts, 2, win_size, piece), jnp.bfloat16),
-        in_specs=[pl.BlockSpec(memory_space=pltpu.SMEM)] + [vmem] * 6,
-        out_specs=vmem,
+        out_shape=jax.ShapeDtypeStruct(slabs, jnp.bfloat16),
+        in_specs=[pl.BlockSpec(memory_space=pltpu.SMEM)] + [anywhere] * 6,
+        out_specs=anywhere,
         scratch_shapes=[
+            pltpu.VMEM(array.shape, array.dtype)
+            for array in (strips, screen_first, screen_second, first, forward, inverse)
+        ]
+        + [
+            pltpu.VMEM(slabs, jnp.bfloat16),
             pltpu.VMEM((2 * sub_size, sub_size), jnp.float32),
-            pltpu.VMEM((2 * sub_size, sub_size), jnp.bfloat16),
+            pltpu.VMEM((sub_local, 2 * sub_size, sub_size), jnp.bfloat16),
             pltpu.VMEM((sub_size, 2 * sub_size), jnp.bfloat16),
+            pltpu.SMEM((sub_local, listing), jnp.int32),
+            pltpu.SemaphoreType.DMA((peer_count,)),
+            pltpu.SemaphoreType.DMA((5,)),
+            pltpu.SemaphoreType.DMA,
         ],
-        compiler_params=pltpu.CompilerParams(vmem_limit_bytes=56 << 20),
+        compiler_params=pltpu.CompilerParams(vmem_limit_bytes=60 << 20),
         name="local",
     )(codes, strips, screen_first, screen_second, first, forward, inverse)
     mine = reduce_partials(partial, peer_count // 2, win_size, piece)

time: 181 us -> 157 us (0.87)
  Pallas kernels: 172 us -> 151 us
  local copies, waits for them, and re-layouts: 6.16 us -> 2.79 us
    pallas_call x1, Pallas kernels: 57.3 us -> 30.8 us  [gathered(): pl.pallas_call(functools.partial(local_body, sub_local, capacity), out_sh...]
    pallas_call x1, Pallas kernels: 53.3 us -> 58.9 us  [reduce_partials(): pl.pallas_call(functools.partial(reduce_body, levels), out_shape=jax.Shap...]
    unnamed x6 -> x4, local copies, waits for them, and re-layouts: 4.93 us -> 1.56 us
where the time goes in v2:
time: 157 us
  Pallas kernels  151 us (96%)
  local copies, waits for them, and re-layouts  2.79 us (2%)
  matrix products  2.41 us (2%)
    pallas_call x1, Pallas kernels, gather_strips(): pl.pallas_call(functools.partial(gather_body, peers), out_shape=[jax.Shap...  61.1 us
    pallas_call x1, Pallas kernels, reduce_partials(): pl.pallas_call(functools.partial(reduce_body, levels), out_shape=jax.Shap...  58.9 us
    pallas_call x1, Pallas kernels, gathered(): pl.pallas_call(functools.partial(local_body, sub_local, capacity), out_sh...  30.8 us

profile of v2, /device:TPU:0, one launch (start us, length us, event | category | flops | bytes accessed | tf_op | source)
XLA Modules:
  0.0 157.0 jit_solution(13590577237117268332)
XLA Ops:
  0.0 0.7 broadcast_compare_fusion
  0.7 0.1 copy.13
  0.8 0.1 eq.37
  1.0 0.8 copy.14
  1.7 0.1 reshape_squeeze.7
  1.9 0.2 convert_reduce_fusion
  2.1 0.8 copy.15
  2.8 0.1 reshape_squeeze.8
  3.0 0.1 select_reduce_fusion
  3.1 0.1 sub.14
  3.2 0.6 pad.4.codes_ref
  3.8 61.1 %gather.1 = (bf16[8,2,64,4096]{3,2,1,0:T(8,128)(2,1)}, s32[8,16,128]{2,1,0:T(8,128)}, bf16[1024,1024]{1,0:T(8,128)(2,1)}, bf16[1024,1024]{1,0:T(8,128)(2,1)}, bf16[1024,1024]{1,0:T(8,128)(2,1)}) custom-call(bf16[2,64,4096]{2,1,0:T(8,128)(2,1)} %strip_ref.1, s32[16,128]{1,0:T(8,128)} %pad.4.codes_ref, bf16[2,512,512]{2,1,0:T(8,128)(2,1)} %constant.26.clone.front_ref, ...), custom_call_target="tpu_custom_call" | custom-call | tf_op jit(solution)/shard_map/gather/pallas_call | solution.py:356
  64.9 30.8 %local.1 = bf16[32,2,64,1024]{3,2,1,0:T(8,128)(2,1)} custom-call(s32[8,16,128]{2,1,0:T(8,128)} %get-tuple-element.10.codes_ref, bf16[8,2,64,4096]{3,2,1,0:T(8,128)(2,1)} %get-tuple-element.11.strips_hbm, bf16[2,512,512]{2,1,0:T(8,128)(2,1)} %screen_first_hbm.1, bf16[2,512,512]{2,1,0:T(8,128)(2,1)} %screen_second_hbm.1, ...), custom_call_target="tpu_custom_call" | custom-call | tf_op jit(solution)/shard_map/local/pallas_call | solution.py:781
  95.7 0.0 copy-start
  95.7 58.9 %reduce.1 = f32[2,64,1024]{2,1,0:T(8,128)} custom-call(bf16[2,4,2,2,2,64,1024]{6,5,4,3,2,1,0:T(8,128)(2,1)} %bitcast.5), custom_call_target="tpu_custom_call" | custom-call | tf_op jit(solution)/shard_map/reduce/pallas_call | solution.py:532
  154.6 0.0 copy-done
  154.6 2.4 %fusion.4 = f32[128,1024]{1,0:T(8,128)} fusion(f32[128,128]{1,0:T(8,128)S(1)} %copy-done, f32[128,1024]{1,0:T(8,128)} %bitcast.6), kind=kOutput, calls=%fused_computation.15 | convolution fusion | flops 201326592 | bytes 1114112 | tf_op jit(solution)/shard_map/dot_general | solution.py:810
  (2 shorter events, 0.0 us)
Async XLA Ops:
  95.7 58.9 %copy-start = (f32[128,128]{1,0:T(8,128)S(1)}, f32[128,128]{1,0:T(8,128)}, u32[]{:S(2)}) copy-start(f32[128,128]{1,0:T(8,128)} %constant.28.clone) | copy-start | bytes 196612

commit v3 on v2

--- a/solution.py
+++ b/solution.py
@@ -173,6 +173,7 @@
 
 GATHER_BYTES = 16 << 20
 UNROLL = 4
+WHOLE, EARLY, LATE = 0, 1, 2
 
 
 def host_table(length):
@@ -259,33 +260,55 @@
     core_peer = (facet, x * 2 + 1 - core)
     corners = [(level * 2 + 1 - y, col) for level in higher]
     meet(z_peers + [y_peer, x_peer, core_peer] + corners)
-    started = []
-
-    def piece(ref, x_at, core_at):
-        return ref.at[x_at, pl.ds(pl.multiple_of(core_at * half, half), half)]
-
-    def send(source, item, x_at, core_at, kind, target):
-        copy = pltpu.make_async_remote_copy(
-            src_ref=piece(source, x_at, core_at),
-            dst_ref=piece(out_ref.at[item], x_at, core_at),
-            send_sem=send_sem.at[len(started)],
-            recv_sem=recv_sem.at[kind, item],
-            device_id=target,
-            device_id_type=pl.DeviceIdType.MESH,
-        )
-        copy.start()
-        started.append(copy)
-
-    def arrived(item, x_at, core_at, kind):
-        pltpu.make_async_copy(
-            piece(out_ref.at[item], x_at, core_at),
-            piece(out_ref.at[item], x_at, core_at),
-            recv_sem.at[kind, item],
-        ).wait()
-
-    send(strip_ref, facet, x, core, 0, y_peer)
-    for target in z_peers:
-        send(strip_ref, facet, x, core, 0, target)
+    sent = []
+
+    def piece(ref, x_at, core_at, span):
+        first = core_at * half + (half // 2 if span == LATE else 0)
+        rows = half if span == WHOLE else half // 2
+        return ref.at[x_at, pl.ds(pl.multiple_of(first, half // 2), rows)]
+
+    def guarded(condition, action):
+        if condition is None:
+            action()
+        else:
+            pl.when(condition)(action)
+
+    def send(condition, source, item, level, x_at, core_at, span, kind, lane, target):
+        def describe():
+            return pltpu.make_async_remote_copy(
+                src_ref=piece(source, x_at, core_at, span),
+                dst_ref=piece(out_ref.at[item], x_at, core_at, span),
+                send_sem=send_sem.at[lane, level],
+                recv_sem=recv_sem.at[kind, item],
+                device_id=target,
+                device_id_type=pl.DeviceIdType.MESH,
+            )
+
+        guarded(condition, lambda: describe().start())
+        sent.append((condition, describe))
+
+    def arrived(condition, item, x_at, core_at, span, kind):
+        def wait():
+            view = piece(out_ref.at[item], x_at, core_at, span)
+            pltpu.make_async_copy(view, view, recv_sem.at[kind, item]).wait()
+
+        guarded(condition, wait)
+
+    def level_sets(distance):
+        if distance == 0:
+            return [(None, z, None, 0, None)]
+        up = ((z + 1) * 2 + y, col)
+        down = ((z - 1) * 2 + y, col)
+        below, above = z - distance >= 0, z + distance < levels
+        return [
+            (below, z - distance, below & (z < levels - 1), 0, up),
+            (above, z + distance, above & (z > 0), 1, down),
+        ]
+
+    send(None, strip_ref, facet, z, x, core, WHOLE, 0, 2, y_peer)
+    send(z < levels - 1, strip_ref, facet, z, x, core, WHOLE, 0, 0, ((z + 1) * 2 + y, col))
+    send(z > 0, strip_ref, facet, z, x, core, WHOLE, 0, 1, ((z - 1) * 2 + y, col))
+    send(None, strip_ref, facet, z, 1 - x, core, EARLY, 4, 7, y_peer)
     codes_sent = []
     for number, target in enumerate([y_peer] + z_peers + corners):
         copy = pltpu.make_async_remote_copy(
@@ -312,33 +335,66 @@
         copy.start()
         kept.append(copy)
 
-    def pass_on(item, kind, x_at):
-        arrived(item, x_at, core, kind)
-        send(out_ref.at[item], item, x_at, core, kind + 2, core_peer)
-
-    order = [z] + higher
-    for number, level in enumerate(order):
-        same, other = level * 2 + y, level * 2 + 1 - y
-        if number > 0:
-            arrived(same, x, core, 0)
-            send(out_ref.at[same], same, x, core, 0, y_peer)
-            send(out_ref.at[same], same, x, core, 1, x_peer)
-            send(out_ref.at[same], same, x, core, 2, core_peer)
-        arrived(other, x, core, 0)
-        send(out_ref.at[other], other, x, core, 1, x_peer)
-        send(out_ref.at[other], other, x, core, 2, core_peer)
-    for number, level in enumerate(order):
-        if number > 0:
-            pass_on(level * 2 + y, 1, 1 - x)
-        pass_on(level * 2 + 1 - y, 1, 1 - x)
-    for number, level in enumerate(order):
-        for item in [level * 2 + y, level * 2 + 1 - y][number == 0 :]:
-            arrived(item, x, 1 - core, 2)
-            arrived(item, 1 - x, 1 - core, 3)
-            pltpu.make_async_copy(
-                all_codes_ref.at[item], all_codes_ref.at[item], code_recv.at[item]
-            ).wait()
-    for copy in started + codes_sent:
+    def along_z(distance):
+        for here, level, onward, lane, target in level_sets(distance):
+            item = level * 2 + y
+            source = out_ref.at[item]
+            arrived(here, item, x, core, WHOLE, 0)
+            send(onward, source, item, level, x, core, WHOLE, 0, lane, target)
+            send(here, source, item, level, x, core, WHOLE, 0, 2, y_peer)
+            send(here, source, item, level, x, core, WHOLE, 1, 3, x_peer)
+            send(here, source, item, level, x, core, WHOLE, 2, 5, core_peer)
+
+    def along_y(distance):
+        for here, level, _, _, _ in level_sets(distance):
+            item = level * 2 + 1 - y
+            source = out_ref.at[item]
+            arrived(here, item, x, core, WHOLE, 0)
+            send(here, source, item, level, x, core, LATE, 1, 4, x_peer)
+            send(here, source, item, level, x, core, WHOLE, 2, 6, core_peer)
+
+    def along_x(distance):
+        for here, level, _, _, _ in level_sets(distance):
+            item = level * 2 + y
+            source = out_ref.at[item]
+            arrived(here, item, 1 - x, core, WHOLE, 1)
+            send(here, source, item, level, 1 - x, core, EARLY, 4, 7, y_peer)
+            send(here, source, item, level, 1 - x, core, WHOLE, 3, 8, core_peer)
+
+    def corner(distance, span, kind, onward, lane):
+        for here, level, _, _, _ in level_sets(distance):
+            item = level * 2 + 1 - y
+            arrived(here, item, 1 - x, core, span, kind)
+            send(here, out_ref.at[item], item, level, 1 - x, core, span, onward, lane, core_peer)
+
+    for distance in range(1, levels + 3):
+        if distance < levels:
+            along_z(distance)
+        if 1 <= distance - 1 < levels:
+            along_x(distance - 1)
+        if 0 <= distance - 1 < levels:
+            along_y(distance - 1)
+        if 0 <= distance - 2 < levels:
+            corner(distance - 2, LATE, 1, 3, 9)
+            corner(distance - 2, EARLY, 4, 5, 10)
+    for distance in range(levels):
+        for here, level, _, _, _ in level_sets(distance):
+            same, other = level * 2 + y, level * 2 + 1 - y
+            if distance > 0:
+                arrived(here, same, x, 1 - core, WHOLE, 2)
+                arrived(here, same, 1 - x, 1 - core, WHOLE, 3)
+            arrived(here, other, x, 1 - core, WHOLE, 2)
+            arrived(here, other, 1 - x, 1 - core, LATE, 3)
+            arrived(here, other, 1 - x, 1 - core, EARLY, 5)
+    for item in [level * 2 + y for level in higher] + [z * 2 + 1 - y] + [
+        level * 2 + 1 - y for level in higher
+    ]:
+        pltpu.make_async_copy(
+            all_codes_ref.at[item], all_codes_ref.at[item], code_recv.at[item]
+        ).wait()
+    for condition, describe in sent:
+        guarded(condition, lambda describe=describe: describe().wait_send())
+    for copy in codes_sent:
         copy.wait_send()
     for copy in kept:
         copy.wait()
@@ -352,7 +408,6 @@
     vmem = pl.BlockSpec(memory_space=pltpu.VMEM)
     anywhere = pl.BlockSpec(memory_space=pl.ANY)
     levels = peers // 2
-    copies = levels + 3 * (levels - 1) + 2 * levels + 2 * levels - 1
     return pl.pallas_call(
         functools.partial(gather_body, peers),
         out_shape=[
@@ -364,8 +419,8 @@
         out_specs=[anywhere] * 5,
         scratch_shapes=[pltpu.VMEM(full, jnp.bfloat16)] * 3
         + [
-            pltpu.SemaphoreType.DMA((copies,)),
-            pltpu.SemaphoreType.DMA((4, peers)),
+            pltpu.SemaphoreType.DMA((11, levels)),
+            pltpu.SemaphoreType.DMA((6, peers)),
             pltpu.SemaphoreType.DMA((peers,)),
             pltpu.SemaphoreType.DMA((peers,)),
             pltpu.SemaphoreType.DMA((5,)),
@@ -550,7 +605,7 @@
             pltpu.SemaphoreType.DMA((levels,)),
         ],
         compiler_params=pltpu.CompilerParams(
-            collective_id=1, has_side_effects=True, vmem_limit_bytes=60 << 20
+            collective_id=1, has_side_effects=True, vmem_limit_bytes=58 << 20
         ),
         name="reduce",
     )(partial.reshape(2, levels, 2, 2, 2, win_size, width))

time: 157 us -> 134 us (0.85)
  Pallas kernels: 151 us -> 128 us
    pallas_call x1, Pallas kernels: 61.1 us -> 47.2 us  [gather_strips(): pl.pallas_call(functools.partial(gather_body, peers), out_shape=[jax.Shap...]
    pallas_call x1, Pallas kernels: 58.9 us -> 50.3 us  [reduce_partials(): pl.pallas_call(functools.partial(reduce_body, levels), out_shape=jax.Shap...]
where the time goes in v3:
time: 134 us
  Pallas kernels  128 us (96%)
  local copies, waits for them, and re-layouts  2.79 us (2%)
  matrix products  2.41 us (2%)
    pallas_call x1, Pallas kernels, reduce_partials(): pl.pallas_call(functools.partial(reduce_body, levels), out_shape=jax.Shap...  50.3 us
    pallas_call x1, Pallas kernels, gather_strips(): pl.pallas_call(functools.partial(gather_body, peers), out_shape=[jax.Shap...  47.2 us
    pallas_call x1, Pallas kernels, gathered(): pl.pallas_call(functools.partial(local_body, sub_local, capacity), out_sh...  30.2 us

profile of v3, /device:TPU:0, one launch (start us, length us, event | category | flops | bytes accessed | tf_op | source)
XLA Modules:
  0.0 134.0 jit_solution(8793404132167687873)
XLA Ops:
  0.0 0.7 broadcast_compare_fusion
  0.7 0.1 copy.13
  0.8 0.1 eq.37
  1.0 0.8 copy.14
  1.7 0.1 reshape_squeeze.7
  1.9 0.2 convert_reduce_fusion
  2.1 0.8 copy.15
  2.8 0.1 reshape_squeeze.8
  3.0 0.1 select_reduce_fusion
  3.1 0.1 sub.14
  3.2 0.6 pad.4.codes_ref
  3.8 47.2 %gather.1 = (bf16[8,2,64,4096]{3,2,1,0:T(8,128)(2,1)}, s32[8,16,128]{2,1,0:T(8,128)}, bf16[1024,1024]{1,0:T(8,128)(2,1)}, bf16[1024,1024]{1,0:T(8,128)(2,1)}, bf16[1024,1024]{1,0:T(8,128)(2,1)}) custom-call(bf16[2,64,4096]{2,1,0:T(8,128)(2,1)} %strip_ref.1, s32[16,128]{1,0:T(8,128)} %pad.4.codes_ref, bf16[2,512,512]{2,1,0:T(8,128)(2,1)} %constant.26.clone.front_ref, ...), custom_call_target="tpu_custom_call" | custom-call | tf_op jit(solution)/shard_map/gather/pallas_call | solution.py:411
  51.1 30.2 %local.1 = bf16[32,2,64,1024]{3,2,1,0:T(8,128)(2,1)} custom-call(s32[8,16,128]{2,1,0:T(8,128)} %get-tuple-element.10.codes_ref, bf16[8,2,64,4096]{3,2,1,0:T(8,128)(2,1)} %get-tuple-element.11.strips_hbm, bf16[2,512,512]{2,1,0:T(8,128)(2,1)} %screen_first_hbm.1, bf16[2,512,512]{2,1,0:T(8,128)(2,1)} %screen_second_hbm.1, ...), custom_call_target="tpu_custom_call" | custom-call | tf_op jit(solution)/shard_map/local/pallas_call | solution.py:836
  81.3 0.0 copy-start
  81.3 50.3 %reduce.1 = f32[2,64,1024]{2,1,0:T(8,128)} custom-call(bf16[2,4,2,2,2,64,1024]{6,5,4,3,2,1,0:T(8,128)(2,1)} %bitcast.5), custom_call_target="tpu_custom_call" | custom-call | tf_op jit(solution)/shard_map/reduce/pallas_call | solution.py:587
  131.6 0.0 copy-done
  131.6 2.4 %fusion.4 = f32[128,1024]{1,0:T(8,128)} fusion(f32[128,128]{1,0:T(8,128)S(1)} %copy-done, f32[128,1024]{1,0:T(8,128)} %bitcast.6), kind=kOutput, calls=%fused_computation.15 | convolution fusion | flops 201326592 | bytes 1114112 | tf_op jit(solution)/shard_map/dot_general | solution.py:865
  (2 shorter events, 0.0 us)
Async XLA Ops:
  81.3 50.3 %copy-start = (f32[128,128]{1,0:T(8,128)S(1)}, f32[128,128]{1,0:T(8,128)}, u32[]{:S(2)}) copy-start(f32[128,128]{1,0:T(8,128)} %constant.28.clone) | copy-start | bytes 196612

commit v4 on v3

--- a/solution.py
+++ b/solution.py
@@ -172,7 +172,7 @@
 
 
 GATHER_BYTES = 16 << 20
-UNROLL = 4
+UNROLL = 8
 WHOLE, EARLY, LATE = 0, 1, 2
 
 
@@ -653,7 +653,7 @@
     parts = out_ref.shape[0] // peers
     base = lax.axis_index("facet") * sub_local
     lane_half = lax.broadcasted_iota(jnp.int32, (win, pair), 1) // win
-    step = size // 2
+    step = size
     loads = [
         pltpu.make_async_copy(strips_hbm.at[peer], strips_ref.at[peer], strip_sem.at[peer])
         for peer in range(peers)
@@ -739,14 +739,14 @@
 
         def left(table_ref):
             for part in range(2):
-                for half in range(2):
+                for half in range(size // step):
                     rows = pl.ds(part * size + half * step, step)
                     flat[pl.ds(half * step, step), pl.ds(part * size, size)] = jnp.dot(
                         table_ref[rows, :], tall[...], preferred_element_type=jnp.float32
                     ).astype(jnp.bfloat16)
 
         def right(table_ref, screen_ref):
-            for half in range(2):
+            for half in range(size // step):
                 rows = pl.ds(half * step, step)
                 product = jnp.dot(flat[rows, :], table_ref[...], preferred_element_type=jnp.float32)
                 real_part, imag_part = product[:, :size], product[:, size:]
@@ -803,14 +803,15 @@
 def entry_codes(owners, live, place, subgrid_count, tile_count):
     win_local = owners.shape[1]
     capacity = max(2, (7 * win_local + 2 * subgrid_count - 1) // (2 * subgrid_count))
-    owner = owners[0].reshape(-1)
-    count = owner.shape[0]
+    joined = jnp.where(live[0] == 1, owners[0] * tile_count + place[0], -1).reshape(-1)
+    owner = jnp.floor_divide(joined, tile_count)
+    count = joined.shape[0]
     window = jnp.arange(count, dtype=jnp.int32) // 3
-    label = window * tile_count + place[0].reshape(-1) + 1
+    label = window * tile_count + (joined - owner * tile_count) + 1
     order = jnp.arange(count, dtype=jnp.int32)
     earlier = (owner[:, None] == owner[None, :]) & (order[None, :] < order[:, None])
     rank = jnp.sum(earlier.astype(jnp.int32), axis=1)
-    slot = jnp.where(live[0].reshape(-1) == 1, owner * capacity + rank, -1)
+    slot = jnp.where(joined >= 0, owner * capacity + rank, -1)
     slots = jnp.arange(subgrid_count * capacity, dtype=jnp.int32)
     hit = slot[None, :] == slots[:, None]
     codes = jnp.sum(jnp.where(hit, label[None, :], 0), axis=1) - 1

time: 134 us -> 131 us (0.978)
  Pallas kernels: 128 us -> 126 us
  local copies, waits for them, and re-layouts: 2.79 us -> 0.93 us
    pallas_call x1, Pallas kernels: 30.2 us -> 27.1 us  [gathered(): pl.pallas_call(functools.partial(local_body, sub_local, capacity), out_sh...]
    unnamed x4 -> x2, local copies, waits for them, and re-layouts: 1.56 us -> 0.01 us
    pallas_call x1, Pallas kernels: 50.3 us -> 51.8 us  [reduce_partials(): pl.pallas_call(functools.partial(reduce_body, levels), out_shape=jax.Shap...]
where the time goes in v4:
time: 131 us
  Pallas kernels  126 us (96%)
  matrix products  2.41 us (2%)
    pallas_call x1, Pallas kernels, reduce_partials(): pl.pallas_call(functools.partial(reduce_body, levels), out_shape=jax.Shap...  51.8 us
    pallas_call x1, Pallas kernels, gather_strips(): pl.pallas_call(functools.partial(gather_body, peers), out_shape=[jax.Shap...  47.2 us
    pallas_call x1, Pallas kernels, gathered(): pl.pallas_call(functools.partial(local_body, sub_local, capacity), out_sh...  27.1 us

profile of v4, /device:TPU:0, one launch (start us, length us, event | category | flops | bytes accessed | tf_op | source)
XLA Modules:
  0.0 130.5 jit_solution(4391001128890212466)
XLA Ops:
  0.0 0.7 compare_select_fusion
  0.7 0.1 copy.11
  0.8 0.1 select_n.61
  1.0 0.2 convert_reduce_fusion
  1.2 0.1 select_reduce_fusion
  1.3 0.1 sub.27
  1.4 0.6 pad.4.codes_ref
  2.0 47.2 %gather.1 = (bf16[8,2,64,4096]{3,2,1,0:T(8,128)(2,1)}, s32[8,16,128]{2,1,0:T(8,128)}, bf16[1024,1024]{1,0:T(8,128)(2,1)}, bf16[1024,1024]{1,0:T(8,128)(2,1)}, bf16[1024,1024]{1,0:T(8,128)(2,1)}) custom-call(bf16[2,64,4096]{2,1,0:T(8,128)(2,1)} %strip_ref.1, s32[16,128]{1,0:T(8,128)} %pad.4.codes_ref, bf16[2,512,512]{2,1,0:T(8,128)(2,1)} %constant.40.clone.front_ref, ...), custom_call_target="tpu_custom_call" | custom-call | tf_op jit(solution)/shard_map/gather/pallas_call | solution.py:411
  49.2 27.1 %local.1 = bf16[32,2,64,1024]{3,2,1,0:T(8,128)(2,1)} custom-call(s32[8,16,128]{2,1,0:T(8,128)} %get-tuple-element.10.codes_ref, bf16[8,2,64,4096]{3,2,1,0:T(8,128)(2,1)} %get-tuple-element.11.strips_hbm, bf16[2,512,512]{2,1,0:T(8,128)(2,1)} %screen_first_hbm.1, bf16[2,512,512]{2,1,0:T(8,128)(2,1)} %screen_second_hbm.1, ...), custom_call_target="tpu_custom_call" | custom-call | tf_op jit(solution)/shard_map/local/pallas_call | solution.py:837
  76.3 0.0 copy-start
  76.3 51.8 %reduce.1 = f32[2,64,1024]{2,1,0:T(8,128)} custom-call(bf16[2,4,2,2,2,64,1024]{6,5,4,3,2,1,0:T(8,128)(2,1)} %bitcast.5), custom_call_target="tpu_custom_call" | custom-call | tf_op jit(solution)/shard_map/reduce/pallas_call | solution.py:587
  128.1 0.0 copy-done
  128.1 2.4 %fusion.4 = f32[128,1024]{1,0:T(8,128)} fusion(f32[128,128]{1,0:T(8,128)S(1)} %copy-done, f32[128,1024]{1,0:T(8,128)} %bitcast.6), kind=kOutput, calls=%fused_computation.19 | convolution fusion | flops 201326592 | bytes 1114112 | tf_op jit(solution)/shard_map/dot_general | solution.py:866
  (3 shorter events, 0.0 us)
Async XLA Ops:
  76.3 51.8 %copy-start = (f32[128,128]{1,0:T(8,128)S(1)}, f32[128,128]{1,0:T(8,128)}, u32[]{:S(2)}) copy-start(f32[128,128]{1,0:T(8,128)} %constant.42.clone) | copy-start | bytes 196612
